TPU v7x, 128 devices: a whole 4x4x4 slice. The times are simulated.
128 devices in a mesh: group: 4 (over x_hi, core), site: 32 (over x_lo, z, y).
Axes of the slice: x: 4 (x_hi: 2, x_lo: 2; x = x_hi * 2 + x_lo), y: 4, z: 4, core: 2. Of those that a mesh axis runs over, the one named last changes fastest.
Arguments:
- residual_in: bfloat16 [32, 64, 128, 128], P('site', 'group'), may hold values from -6 to 6
- self_block: bfloat16 [32, 64, 64, 128], P('site'), may hold values from -0.25 to 0.25
- hop_blocks: bfloat16 [32, 64, 8, 64, 128], P('site'), may hold values from -0.1875 to 0.1875
Outputs:
- correction: float32 [32, 64, 128, 128], P('site', 'group')
- residual_out: float32 [32, 64, 128, 128], P('site', 'group')
All inputs are finite; a program needn't handle non-finite values.
Results may differ from a plain program's by a relative error of at most 0.017.
Values may be sent and summed in bfloat16 or wider, within the bound.
A program may use at most 64 MiB of HBM per device.

v0:
```python
import jax
import jax.numpy as jnp
from jax import lax
from jax.sharding import PartitionSpec as P

XP = 2
LY = 4
LZ = 2
STEPS = 4


diagonal_shift = 1.5
center_value = 1.5
half_width = 1.0


def extended(value, sides, width):
    for axis, dim in sides:
        size, length = (lax.axis_size(axis), value.shape[dim])
        up = [(i, (i + 1) % size) for i in range(size)]
        down = [(j, i) for i, j in up]
        last = lax.slice_in_dim(value, length - width, length, axis=dim)
        leading = lax.slice_in_dim(value, 0, width, axis=dim)
        before = lax.ppermute(last, axis, up)
        after = lax.ppermute(leading, axis, down)
        value = jnp.concatenate([before, value, after], axis=dim)
    return value


def paired(vector):
    half = vector.shape[-1] // 2
    real_part = vector[..., :half]
    imag_part = vector[..., half:]
    conjugate = jnp.concatenate([real_part, -imag_part], axis=-1)
    swapped = jnp.concatenate([imag_part, real_part], axis=-1)
    return jnp.concatenate([conjugate, swapped], axis=-2)


def apply_blocks(vector, around, own_self, own_hops):
    count = vector.shape[2]
    own_out = jnp.einsum(
        "tsab,tskb->tska", own_self, paired(vector), preferred_element_type=jnp.float32
    )
    hop_out = jnp.einsum(
        "tsmab,tsmkb->tska", own_hops, paired(around), preferred_element_type=jnp.float32
    )
    total = own_out + hop_out
    mixed = jnp.concatenate([total[:, :, :count], total[:, :, count:]], axis=-1)
    return diagonal_shift * vector.astype(jnp.float32) + mixed


def body(residual_in, self_block, hop_blocks):
    slices = residual_in.shape[0]
    span = XP * LY * LZ
    start = lax.axis_index("group") * span
    own_self = lax.dynamic_slice_in_dim(self_block, start, span, 1)
    own_hops = lax.dynamic_slice_in_dim(hop_blocks, start, span, 1)
    residual = residual_in.astype(jnp.float32)
    correction = jnp.zeros(residual.shape, jnp.float32)
    ratio = half_width / center_value
    direction = residual / center_value
    for number in range(STEPS):
        if number > 0:
            ratio_next = 1.0 / (2.0 * center_value / half_width - ratio)
            direction = ratio_next * ratio * direction + 2.0 * ratio_next / half_width * residual
            ratio = ratio_next
        correction = correction + direction
        sent = direction.astype(jnp.bfloat16)
        flat_shape = sent.shape
        grid = sent.reshape((slices, XP, LY, LZ) + flat_shape[2:])
        padded = extended(grid, (("group", 1), ("site", 0)), 1)
        center = padded[1:-1, 1:-1]
        moved = [padded[1:-1, 2:], padded[1:-1, :-2]]
        for axis_number in (2, 3):
            moved.append(jnp.roll(center, -1, axis_number))
            moved.append(jnp.roll(center, 1, axis_number))
        moved.append(padded[2:, 1:-1])
        moved.append(padded[:-2, 1:-1])
        residual = residual - apply_blocks(
            sent,
            jnp.stack([piece.reshape(flat_shape) for piece in moved], axis=2),
            own_self,
            own_hops,
        )
    return (correction, residual)


def solution(mesh):
    return jax.shard_map(
        body,
        mesh=mesh,
        in_specs=(
            P("site", "group", None, None),
            P("site", None, None, None),
            P("site", None, None, None, None),
        ),
        out_specs=(P("site", "group", None, None), P("site", "group", None, None)),
        check_vma=False,
    )
```

profile of v0, /device:TPU:1, one launch (start us, length us, event | category | flops | bytes accessed | tf_op | source)
XLA Modules:
  0.0 281.3 jit_solution(6915172860090646498)
XLA Ops:
  3.0 4.1 %collective-permute-start.1 = (bf16[1,1,4,2,128,128]{4,5,3,2,1,0:T(8,128)(2,1)}, bf16[1,1,4,2,128,128]{4,5,3,2,1,0:T(8,128)(2,1)S(1)}, u32[]{:S(2)}, u32[]{:S(2)}) collective-permute-start(bf16[1,1,4,2,128,128]{4,5,3,2,1,0:T(8,128)(2,1)} %get-tuple-element.78), channel_id=1, source_target_pairs={{0,32},{32,64},{64,96},{96,0},{1,33},{33,65},{65,97},{97,1},{2,34}... | collective-permute-start | bytes 786440 | tf_op jit(solution)/shard_map/ppermute | solution.py:24
  16.8 6.6 %collective-permute-start.2 = (bf16[1,4,4,2,128,128]{4,5,3,2,1,0:T(8,128)(2,1)}, bf16[1,4,4,2,128,128]{4,5,3,2,1,0:T(8,128)(2,1)}, u32[]{:S(2)}, u32[]{:S(2)}) collective-permute-start(bf16[1,4,4,2,128,128]{4,5,3,2,1,0:T(8,128)(2,1)} %pad_maximum_fusion), channel_id=1, source_target_pairs={{1,0},{2,1},{3,2},{4,3},{5,4},{6,5},{7,6},{8,7},{9,8},{10,9},{11,1... | collective-permute-start | bytes 3145736 | tf_op jit(solution)/shard_map/ppermute | solution.py:25
  27.8 2.1 copy.16
  37.5 8.8 %collective-permute-done.2 = bf16[1,4,4,2,128,128]{4,5,3,2,1,0:T(8,128)(2,1)} collective-permute-done((bf16[1,4,4,2,128,128]{4,5,3,2,1,0:T(8,128)(2,1)}, bf16[1,4,4,2,128,128]{4,5,3,2,1,0:T(8,128)(2,1)}, u32[]{:S(2)}, u32[]{:S(2)}) %collective-permute-start.2) | collective-permute-done | bytes 1048608 | tf_op jit(solution)/shard_map/ppermute | solution.py:25
  47.7 5.2 %collective-permute-done.3 = bf16[1,4,4,2,128,128]{4,5,3,2,1,0:T(8,128)(2,1)} collective-permute-done((bf16[1,4,4,2,128,128]{4,5,3,2,1,0:T(8,128)(2,1)}, bf16[1,4,4,2,128,128]{4,5,3,2,1,0:T(8,128)(2,1)}, u32[]{:S(2)}, u32[]{:S(2)}) %collective-permute-start.3) | collective-permute-done | bytes 1048608 | tf_op jit(solution)/shard_map/ppermute | solution.py:24
  56.1 5.2 %slice_negate_fusion.7 = (bf16[1,16,8,128,64]{4,3,2,1,0:T(8,128)(2,1)S(1)}, bf16[1,16,8,128,64]{4,3,2,1,0:T(8,128)(2,1)S(1)}, bf16[1,16,8,128,64]{4,3,2,1,0:T(8,128)(2,1)S(1)}) fusion(bf16[1,16,8,128,128]{4,3,2,1,0:T(8,128)(2,1)} %constant_dynamic-update-slice_fusion), kind=kLoop, calls=%fused_computation.186 | loop fusion | flops 1048576 | bytes 10485760 | tf_op jit(solution)/shard_map/neg | solution.py:34
  61.3 7.0 %fusion.41 = f32[16,256,64]{1,2,0:T(8,128)S(1)} fusion(bf16[1,16,8,128,64]{4,3,2,1,0:T(8,128)(2,1)S(1)} %get-tuple-element.17, bf16[1,16,8,128,64]{4,3,2,1,0:T(8,128)(2,1)S(1)} %get-tuple-element.16, bf16[1,16,8,128,64]{4,3,2,1,0:T(8,128)(2,1)S(1)} %get-tuple-element.15, bf16[1,64,8,64,128]{4,3,2,1,0:T(8,128)(2,1)} %param.5, s32[]{:T(128)S(6)} %select_n.4), kind=kOutput, calls=%fused_computation.42 | convolution fusion | flops 570425344 | bytes 9437188 | tf_op jit(solution)/shard_map/tsmab,tsmkb->tska/dot_general | solution.py:44
  70.8 2.8 collective-permute-start.5
  83.3 2.1 pad_maximum_fusion.1
  87.7 2.1 pad_maximum_fusion.8
  89.8 2.1 copy.23
  103.8 5.7 %collective-permute-done.6 = bf16[1,4,4,2,128,128]{4,5,3,2,1,0:T(8,128)(2,1)} collective-permute-done((bf16[1,4,4,2,128,128]{4,5,3,2,1,0:T(8,128)(2,1)}, bf16[1,4,4,2,128,128]{4,5,3,2,1,0:T(8,128)(2,1)}, u32[]{:S(2)}, u32[]{:S(2)}) %collective-permute-start.6) | collective-permute-done | bytes 1048608 | tf_op jit(solution)/shard_map/ppermute | solution.py:25
  119.9 5.2 %slice_negate_fusion.6 = (bf16[1,16,8,128,64]{4,3,2,1,0:T(8,128)(2,1)S(1)}, bf16[1,16,8,128,64]{4,3,2,1,0:T(8,128)(2,1)S(1)}, bf16[1,16,8,128,64]{4,3,2,1,0:T(8,128)(2,1)S(1)}) fusion(bf16[1,16,8,128,128]{4,3,2,1,0:T(8,128)(2,1)} %constant_dynamic-update-slice_fusion.8), kind=kLoop, calls=%fused_computation.185 | loop fusion | flops 1048576 | bytes 10485760 | tf_op jit(solution)/shard_map/neg | solution.py:34
  125.2 7.0 %fusion.38 = f32[16,256,64]{1,2,0:T(8,128)S(1)} fusion(bf16[1,16,8,128,64]{4,3,2,1,0:T(8,128)(2,1)S(1)} %get-tuple-element.14, bf16[1,16,8,128,64]{4,3,2,1,0:T(8,128)(2,1)S(1)} %get-tuple-element.13, bf16[1,16,8,128,64]{4,3,2,1,0:T(8,128)(2,1)S(1)} %get-tuple-element.12, bf16[1,64,8,64,128]{4,3,2,1,0:T(8,128)(2,1)} %param.5, s32[]{:T(128)S(6)} %select_n.4), kind=kOutput, calls=%fused_computation.41 | convolution fusion | flops 570425344 | bytes 9437188 | tf_op jit(solution)/shard_map/tsmab,tsmkb->tska/dot_general | solution.py:44
  135.6 4.3 %collective-permute-start.9 = (bf16[1,1,4,2,128,128]{4,5,3,2,1,0:T(8,128)(2,1)}, bf16[1,1,4,2,128,128]{4,5,3,2,1,0:T(8,128)(2,1)}, u32[]{:S(2)}, u32[]{:S(2)}) collective-permute-start(bf16[1,1,4,2,128,128]{4,5,3,2,1,0:T(8,128)(2,1)} %get-tuple-element.52), channel_id=1, source_target_pairs={{0,32},{32,64},{64,96},{96,0},{1,33},{33,65},{65,97},{97,1},{2,34}... | collective-permute-start | bytes 786440 | tf_op jit(solution)/shard_map/ppermute | solution.py:24
  149.7 2.1 pad_maximum_fusion.2
  151.8 2.6 collective-permute-start.10
  155.3 2.1 pad_maximum_fusion.6
  171.3 3.9 %collective-permute-done.10 = bf16[1,4,4,2,128,128]{4,5,3,2,1,0:T(8,128)(2,1)} collective-permute-done((bf16[1,4,4,2,128,128]{4,5,3,2,1,0:T(8,128)(2,1)}, bf16[1,4,4,2,128,128]{4,5,3,2,1,0:T(8,128)(2,1)}, u32[]{:S(2)}, u32[]{:S(2)}) %collective-permute-start.10) | collective-permute-done | bytes 1048608 | tf_op jit(solution)/shard_map/ppermute | solution.py:25
  178.4 2.7 collective-permute-done.11
  188.0 5.2 %slice_negate_fusion.5 = (bf16[1,16,8,128,64]{4,3,2,1,0:T(8,128)(2,1)S(1)}, bf16[1,16,8,128,64]{4,3,2,1,0:T(8,128)(2,1)S(1)}, bf16[1,16,8,128,64]{4,3,2,1,0:T(8,128)(2,1)S(1)}) fusion(bf16[1,16,8,128,128]{4,3,2,1,0:T(8,128)(2,1)} %constant_dynamic-update-slice_fusion.16), kind=kLoop, calls=%fused_computation.184 | loop fusion | flops 1048576 | bytes 10485760 | tf_op jit(solution)/shard_map/neg | solution.py:34
  193.2 7.0 %fusion.35 = f32[16,256,64]{1,2,0:T(8,128)S(1)} fusion(bf16[1,16,8,128,64]{4,3,2,1,0:T(8,128)(2,1)S(1)} %get-tuple-element.11, bf16[1,16,8,128,64]{4,3,2,1,0:T(8,128)(2,1)S(1)} %get-tuple-element.10, bf16[1,16,8,128,64]{4,3,2,1,0:T(8,128)(2,1)S(1)} %get-tuple-element.9, bf16[1,64,8,64,128]{4,3,2,1,0:T(8,128)(2,1)} %param.5, s32[]{:T(128)S(6)} %select_n.4), kind=kOutput, calls=%fused_computation.40 | convolution fusion | flops 570425344 | bytes 9437188 | tf_op jit(solution)/shard_map/tsmab,tsmkb->tska/dot_general | solution.py:44
  204.8 5.8 %collective-permute-start.13 = (bf16[1,1,4,2,128,128]{4,5,3,2,1,0:T(8,128)(2,1)}, bf16[1,1,4,2,128,128]{4,5,3,2,1,0:T(8,128)(2,1)}, u32[]{:S(2)}, u32[]{:S(2)}) collective-permute-start(bf16[1,1,4,2,128,128]{4,5,3,2,1,0:T(8,128)(2,1)} %get-tuple-element.39), channel_id=1, source_target_pairs={{0,32},{32,64},{64,96},{96,0},{1,33},{33,65},{65,97},{97,1},{2,34}... | collective-permute-start | bytes 786440 | tf_op jit(solution)/shard_map/ppermute | solution.py:24
  220.2 2.1 pad_maximum_fusion.3
  222.4 2.6 collective-permute-start.14
  225.8 2.2 pad_maximum_fusion.4
  242.0 4.5 %collective-permute-done.14 = bf16[1,4,4,2,128,128]{4,5,3,2,1,0:T(8,128)(2,1)} collective-permute-done((bf16[1,4,4,2,128,128]{4,5,3,2,1,0:T(8,128)(2,1)}, bf16[1,4,4,2,128,128]{4,5,3,2,1,0:T(8,128)(2,1)}, u32[]{:S(2)}, u32[]{:S(2)}) %collective-permute-start.14) | collective-permute-done | bytes 1048608 | tf_op jit(solution)/shard_map/ppermute | solution.py:25
  260.3 5.2 %slice_negate_fusion.4 = (bf16[1,16,8,128,64]{4,3,2,1,0:T(8,128)(2,1)S(1)}, bf16[1,16,8,128,64]{4,3,2,1,0:T(8,128)(2,1)S(1)}, bf16[1,16,8,128,64]{4,3,2,1,0:T(8,128)(2,1)S(1)}) fusion(bf16[1,16,8,128,128]{4,3,2,1,0:T(8,128)(2,1)} %constant_dynamic-update-slice_fusion.24), kind=kLoop, calls=%fused_computation.183 | loop fusion | flops 1048576 | bytes 10485760 | tf_op jit(solution)/shard_map/neg | solution.py:34
  265.6 7.0 %fusion.32 = f32[16,256,64]{1,2,0:T(8,128)S(1)} fusion(bf16[1,16,8,128,64]{4,3,2,1,0:T(8,128)(2,1)S(1)} %get-tuple-element.8, bf16[1,16,8,128,64]{4,3,2,1,0:T(8,128)(2,1)S(1)} %get-tuple-element.7, bf16[1,16,8,128,64]{4,3,2,1,0:T(8,128)(2,1)S(1)} %get-tuple-element.6, bf16[1,64,8,64,128]{4,3,2,1,0:T(8,128)(2,1)} %param.5, s32[]{:T(128)S(6)} %select_n.4), kind=kOutput, calls=%fused_computation.39 | convolution fusion | flops 570425344 | bytes 9437188 | tf_op jit(solution)/shard_map/tsmab,tsmkb->tska/dot_general | solution.py:44
  274.2 2.1 fusion.83
  276.3 2.5 copy.46
  278.8 2.5 copy.47
  (171 shorter events, 147.4 us)
Async XLA Ops:
  0.6 67.7 %copy-start = (bf16[1,64,64,128]{3,2,1,0:T(8,128)(2,1)S(1)}, bf16[1,64,64,128]{3,2,1,0:T(8,128)(2,1)}, u32[]{:S(2)}) copy-start(bf16[1,64,64,128]{3,2,1,0:T(8,128)(2,1)} %param.4) | copy-start | bytes 3145732
  3.0 9.9 %collective-permute-start.1 = (bf16[1,1,4,2,128,128]{4,5,3,2,1,0:T(8,128)(2,1)}, bf16[1,1,4,2,128,128]{4,5,3,2,1,0:T(8,128)(2,1)S(1)}, u32[]{:S(2)}, u32[]{:S(2)}) collective-permute-start(bf16[1,1,4,2,128,128]{4,5,3,2,1,0:T(8,128)(2,1)} %get-tuple-element.78), channel_id=1, source_target_pairs={{0,32},{32,64},{64,96},{96,0},{1,33},{33,65},{65,97},{97,1},{2,34}... | collective-permute-start | bytes 786440 | tf_op jit(solution)/shard_map/ppermute | solution.py:24
  7.2 7.6 %collective-permute-start = (bf16[1,1,4,2,128,128]{4,5,3,2,1,0:T(8,128)(2,1)}, bf16[1,1,4,2,128,128]{4,5,3,2,1,0:T(8,128)(2,1)}, u32[]{:S(2)}, u32[]{:S(2)}) collective-permute-start(bf16[1,1,4,2,128,128]{4,5,3,2,1,0:T(8,128)(2,1)} %get-tuple-element.79), channel_id=1, source_target_pairs={{32,0},{64,32},{96,64},{0,96},{33,1},{65,33},{97,65},{1,97},{34,2}... | collective-permute-start | bytes 786440 | tf_op jit(solution)/shard_map/ppermute | solution.py:25
  16.8 29.5 %collective-permute-start.2 = (bf16[1,4,4,2,128,128]{4,5,3,2,1,0:T(8,128)(2,1)}, bf16[1,4,4,2,128,128]{4,5,3,2,1,0:T(8,128)(2,1)}, u32[]{:S(2)}, u32[]{:S(2)}) collective-permute-start(bf16[1,4,4,2,128,128]{4,5,3,2,1,0:T(8,128)(2,1)} %pad_maximum_fusion), channel_id=1, source_target_pairs={{1,0},{2,1},{3,2},{4,3},{5,4},{6,5},{7,6},{8,7},{9,8},{10,9},{11,1... | collective-permute-start | bytes 3145736 | tf_op jit(solution)/shard_map/ppermute | solution.py:25
  23.4 29.4 %collective-permute-start.3 = (bf16[1,4,4,2,128,128]{4,5,3,2,1,0:T(8,128)(2,1)}, bf16[1,4,4,2,128,128]{4,5,3,2,1,0:T(8,128)(2,1)}, u32[]{:S(2)}, u32[]{:S(2)}) collective-permute-start(bf16[1,4,4,2,128,128]{4,5,3,2,1,0:T(8,128)(2,1)} %pad_maximum_fusion), channel_id=1, source_target_pairs={{0,1},{1,2},{2,3},{3,4},{4,5},{5,6},{6,7},{7,8},{8,9},{9,10},{10,1... | collective-permute-start | bytes 3145736 | tf_op jit(solution)/shard_map/ppermute | solution.py:24
  61.3 7.1 %copy-start.11 = (bf16[1,16,128,64]{2,3,1,0:T(8,128)(2,1)S(1)}, bf16[1,16,128,64]{2,3,1,0:T(8,128)(2,1)}, u32[]{:S(2)}) copy-start(bf16[1,16,128,64]{2,3,1,0:T(8,128)(2,1)} %get-tuple-element.67) | copy-start | bytes 786436
  61.3 7.1 %copy-start.12 = (bf16[1,16,128,64]{2,3,1,0:T(8,128)(2,1)S(1)}, bf16[1,16,128,64]{2,3,1,0:T(8,128)(2,1)}, u32[]{:S(2)}) copy-start(bf16[1,16,128,64]{2,3,1,0:T(8,128)(2,1)} %get-tuple-element.68) | copy-start | bytes 786436
  61.3 7.1 %copy-start.13 = (bf16[1,16,128,64]{2,3,1,0:T(8,128)(2,1)S(1)}, bf16[1,16,128,64]{2,3,1,0:T(8,128)(2,1)}, u32[]{:S(2)}) copy-start(bf16[1,16,128,64]{2,3,1,0:T(8,128)(2,1)} %get-tuple-element.69) | copy-start | bytes 786436
  70.8 12.5 %collective-permute-start.5 = (bf16[1,1,4,2,128,128]{4,5,3,2,1,0:T(8,128)(2,1)}, bf16[1,1,4,2,128,128]{4,5,3,2,1,0:T(8,128)(2,1)}, u32[]{:S(2)}, u32[]{:S(2)}) collective-permute-start(bf16[1,1,4,2,128,128]{4,5,3,2,1,0:T(8,128)(2,1)} %get-tuple-element.65), channel_id=1, source_target_pairs={{0,32},{32,64},{64,96},{96,0},{1,33},{33,65},{65,97},{97,1},{2,34}... | collective-permute-start | bytes 786440 | tf_op jit(solution)/shard_map/ppermute | solution.py:24
  73.6 9.7 %collective-permute-start.4 = (bf16[1,1,4,2,128,128]{4,5,3,2,1,0:T(8,128)(2,1)}, bf16[1,1,4,2,128,128]{4,5,3,2,1,0:T(8,128)(2,1)}, u32[]{:S(2)}, u32[]{:S(2)}) collective-permute-start(bf16[1,1,4,2,128,128]{4,5,3,2,1,0:T(8,128)(2,1)} %get-tuple-element.66), channel_id=1, source_target_pairs={{32,0},{64,32},{96,64},{0,96},{33,1},{65,33},{97,65},{1,97},{34,2}... | collective-permute-start | bytes 786440 | tf_op jit(solution)/shard_map/ppermute | solution.py:25
  85.4 24.1 %collective-permute-start.6 = (bf16[1,4,4,2,128,128]{4,5,3,2,1,0:T(8,128)(2,1)}, bf16[1,4,4,2,128,128]{4,5,3,2,1,0:T(8,128)(2,1)}, u32[]{:S(2)}, u32[]{:S(2)}) collective-permute-start(bf16[1,4,4,2,128,128]{4,5,3,2,1,0:T(8,128)(2,1)} %pad_maximum_fusion.1), channel_id=1, source_target_pairs={{1,0},{2,1},{3,2},{4,3},{5,4},{6,5},{7,6},{8,7},{9,8},{10,9},{11,1... | collective-permute-start | bytes 3145736 | tf_op jit(solution)/shard_map/ppermute | solution.py:25
  85.6 27.5 %collective-permute-start.7 = (bf16[1,4,4,2,128,128]{4,5,3,2,1,0:T(8,128)(2,1)}, bf16[1,4,4,2,128,128]{4,5,3,2,1,0:T(8,128)(2,1)}, u32[]{:S(2)}, u32[]{:S(2)}) collective-permute-start(bf16[1,4,4,2,128,128]{4,5,3,2,1,0:T(8,128)(2,1)} %pad_maximum_fusion.1), channel_id=1, source_target_pairs={{0,1},{1,2},{2,3},{3,4},{4,5},{5,6},{6,7},{7,8},{8,9},{9,10},{10,1... | collective-permute-start | bytes 3145736 | tf_op jit(solution)/shard_map/ppermute | solution.py:24
  89.8 12.2 %copy-start.7 = (bf16[1,2,4,2,128,128]{5,4,3,2,1,0:T(8,128)(2,1)S(1)}, bf16[1,2,4,2,128,128]{5,4,3,2,1,0:T(8,128)(2,1)}, u32[]{:S(2)}) copy-start(bf16[1,2,4,2,128,128]{5,4,3,2,1,0:T(8,128)(2,1)} %copy.27) | copy-start | bytes 1572868
  125.1 7.0 %copy-start.14 = (bf16[1,16,128,64]{2,3,1,0:T(8,128)(2,1)S(1)}, bf16[1,16,128,64]{2,3,1,0:T(8,128)(2,1)}, u32[]{:S(2)}) copy-start(bf16[1,16,128,64]{2,3,1,0:T(8,128)(2,1)} %get-tuple-element.55) | copy-start | bytes 786436
  125.2 7.0 %copy-start.15 = (bf16[1,16,128,64]{2,3,1,0:T(8,128)(2,1)S(1)}, bf16[1,16,128,64]{2,3,1,0:T(8,128)(2,1)}, u32[]{:S(2)}) copy-start(bf16[1,16,128,64]{2,3,1,0:T(8,128)(2,1)} %get-tuple-element.56) | copy-start | bytes 786436
  132.6 1.4 copy-start.4
  135.6 14.0 %collective-permute-start.9 = (bf16[1,1,4,2,128,128]{4,5,3,2,1,0:T(8,128)(2,1)}, bf16[1,1,4,2,128,128]{4,5,3,2,1,0:T(8,128)(2,1)}, u32[]{:S(2)}, u32[]{:S(2)}) collective-permute-start(bf16[1,1,4,2,128,128]{4,5,3,2,1,0:T(8,128)(2,1)} %get-tuple-element.52), channel_id=1, source_target_pairs={{0,32},{32,64},{64,96},{96,0},{1,33},{33,65},{65,97},{97,1},{2,34}... | collective-permute-start | bytes 786440 | tf_op jit(solution)/shard_map/ppermute | solution.py:24
  140.0 9.7 %collective-permute-start.8 = (bf16[1,1,4,2,128,128]{4,5,3,2,1,0:T(8,128)(2,1)}, bf16[1,1,4,2,128,128]{4,5,3,2,1,0:T(8,128)(2,1)}, u32[]{:S(2)}, u32[]{:S(2)}) collective-permute-start(bf16[1,1,4,2,128,128]{4,5,3,2,1,0:T(8,128)(2,1)} %get-tuple-element.53), channel_id=1, source_target_pairs={{32,0},{64,32},{96,64},{0,96},{33,1},{65,33},{97,65},{1,97},{34,2}... | collective-permute-start | bytes 786440 | tf_op jit(solution)/shard_map/ppermute | solution.py:25
  151.8 23.4 %collective-permute-start.10 = (bf16[1,4,4,2,128,128]{4,5,3,2,1,0:T(8,128)(2,1)}, bf16[1,4,4,2,128,128]{4,5,3,2,1,0:T(8,128)(2,1)}, u32[]{:S(2)}, u32[]{:S(2)}) collective-permute-start(bf16[1,4,4,2,128,128]{4,5,3,2,1,0:T(8,128)(2,1)} %pad_maximum_fusion.2), channel_id=1, source_target_pairs={{1,0},{2,1},{3,2},{4,3},{5,4},{6,5},{7,6},{8,7},{9,8},{10,9},{11,1... | collective-permute-start | bytes 3145736 | tf_op jit(solution)/shard_map/ppermute | solution.py:25
  154.4 26.7 %collective-permute-start.11 = (bf16[1,4,4,2,128,128]{4,5,3,2,1,0:T(8,128)(2,1)}, bf16[1,4,4,2,128,128]{4,5,3,2,1,0:T(8,128)(2,1)}, u32[]{:S(2)}, u32[]{:S(2)}) collective-permute-start(bf16[1,4,4,2,128,128]{4,5,3,2,1,0:T(8,128)(2,1)} %pad_maximum_fusion.2), channel_id=1, source_target_pairs={{0,1},{1,2},{2,3},{3,4},{4,5},{5,6},{6,7},{7,8},{8,9},{9,10},{10,1... | collective-permute-start | bytes 3145736 | tf_op jit(solution)/shard_map/ppermute | solution.py:24
  157.4 12.1 %copy-start.8 = (bf16[1,2,4,2,128,128]{5,4,3,2,1,0:T(8,128)(2,1)S(1)}, bf16[1,2,4,2,128,128]{5,4,3,2,1,0:T(8,128)(2,1)}, u32[]{:S(2)}) copy-start(bf16[1,2,4,2,128,128]{5,4,3,2,1,0:T(8,128)(2,1)} %copy.35) | copy-start | bytes 1572868
  193.2 7.0 %copy-start.16 = (bf16[1,16,128,64]{2,3,1,0:T(8,128)(2,1)S(1)}, bf16[1,16,128,64]{2,3,1,0:T(8,128)(2,1)}, u32[]{:S(2)}) copy-start(bf16[1,16,128,64]{2,3,1,0:T(8,128)(2,1)} %get-tuple-element.42) | copy-start | bytes 786436
  193.2 7.0 %copy-start.17 = (bf16[1,16,128,64]{2,3,1,0:T(8,128)(2,1)S(1)}, bf16[1,16,128,64]{2,3,1,0:T(8,128)(2,1)}, u32[]{:S(2)}) copy-start(bf16[1,16,128,64]{2,3,1,0:T(8,128)(2,1)} %get-tuple-element.43) | copy-start | bytes 786436
  204.8 15.5 %collective-permute-start.13 = (bf16[1,1,4,2,128,128]{4,5,3,2,1,0:T(8,128)(2,1)}, bf16[1,1,4,2,128,128]{4,5,3,2,1,0:T(8,128)(2,1)}, u32[]{:S(2)}, u32[]{:S(2)}) collective-permute-start(bf16[1,1,4,2,128,128]{4,5,3,2,1,0:T(8,128)(2,1)} %get-tuple-element.39), channel_id=1, source_target_pairs={{0,32},{32,64},{64,96},{96,0},{1,33},{33,65},{65,97},{97,1},{2,34}... | collective-permute-start | bytes 786440 | tf_op jit(solution)/shard_map/ppermute | solution.py:24
  210.6 9.7 %collective-permute-start.12 = (bf16[1,1,4,2,128,128]{4,5,3,2,1,0:T(8,128)(2,1)}, bf16[1,1,4,2,128,128]{4,5,3,2,1,0:T(8,128)(2,1)}, u32[]{:S(2)}, u32[]{:S(2)}) collective-permute-start(bf16[1,1,4,2,128,128]{4,5,3,2,1,0:T(8,128)(2,1)} %get-tuple-element.40), channel_id=1, source_target_pairs={{32,0},{64,32},{96,64},{0,96},{33,1},{65,33},{97,65},{1,97},{34,2}... | collective-permute-start | bytes 786440 | tf_op jit(solution)/shard_map/ppermute | solution.py:25
  222.4 24.1 %collective-permute-start.14 = (bf16[1,4,4,2,128,128]{4,5,3,2,1,0:T(8,128)(2,1)}, bf16[1,4,4,2,128,128]{4,5,3,2,1,0:T(8,128)(2,1)}, u32[]{:S(2)}, u32[]{:S(2)}) collective-permute-start(bf16[1,4,4,2,128,128]{4,5,3,2,1,0:T(8,128)(2,1)} %pad_maximum_fusion.3), channel_id=1, source_target_pairs={{1,0},{2,1},{3,2},{4,3},{5,4},{6,5},{7,6},{8,7},{9,8},{10,9},{11,1... | collective-permute-start | bytes 3145736 | tf_op jit(solution)/shard_map/ppermute | solution.py:25
  225.0 27.5 %collective-permute-start.15 = (bf16[1,4,4,2,128,128]{4,5,3,2,1,0:T(8,128)(2,1)}, bf16[1,4,4,2,128,128]{4,5,3,2,1,0:T(8,128)(2,1)}, u32[]{:S(2)}, u32[]{:S(2)}) collective-permute-start(bf16[1,4,4,2,128,128]{4,5,3,2,1,0:T(8,128)(2,1)} %pad_maximum_fusion.3), channel_id=1, source_target_pairs={{0,1},{1,2},{2,3},{3,4},{4,5},{5,6},{6,7},{7,8},{8,9},{9,10},{10,1... | collective-permute-start | bytes 3145736 | tf_op jit(solution)/shard_map/ppermute | solution.py:24
  232.1 8.0 %copy-start.9 = (bf16[1,2,4,2,128,128]{5,4,3,2,1,0:T(8,128)(2,1)S(1)}, bf16[1,2,4,2,128,128]{5,4,3,2,1,0:T(8,128)(2,1)}, u32[]{:S(2)}) copy-start(bf16[1,2,4,2,128,128]{5,4,3,2,1,0:T(8,128)(2,1)} %copy.43) | copy-start | bytes 1572868
  265.6 7.1 %copy-start.18 = (bf16[1,16,128,64]{2,3,1,0:T(8,128)(2,1)S(1)}, bf16[1,16,128,64]{2,3,1,0:T(8,128)(2,1)}, u32[]{:S(2)}) copy-start(bf16[1,16,128,64]{2,3,1,0:T(8,128)(2,1)} %get-tuple-element.29) | copy-start | bytes 786436
  265.6 7.1 %copy-start.19 = (bf16[1,16,128,64]{2,3,1,0:T(8,128)(2,1)S(1)}, bf16[1,16,128,64]{2,3,1,0:T(8,128)(2,1)}, u32[]{:S(2)}) copy-start(bf16[1,16,128,64]{2,3,1,0:T(8,128)(2,1)} %get-tuple-element.30) | copy-start | bytes 786436
  272.6 1.2 copy-start.6
  272.6 1.5 copy-start.10
  (4 other events, 4.1 us)
where the time goes:
time: 286 us; the launch traced here: 281 us
  local copies, waits for them, and re-layouts  127 us (44%)
  other arithmetic  58.1 us (20%)
  waiting for transfers between devices  35.1 us (12%)
  starting transfers between devices  30.4 us (11%)
  matrix products  29.2 us (10%)
    unnamed x71, local copies, waits for them, and re-layouts  51.1 us
    dot_general x4, matrix products, apply_blocks(): jnp.einsum('tsmab,tsmkb->tska', own_hops, paired(around), preferred_eleme...  28 us
    ppermute x8, waiting for transfers between devices, extended(): after = lax.ppermute(leading, axis, down)  24.7 us
    neg x8, other arithmetic, paired(): conjugate = jnp.concatenate([real_part, -imag_part], axis=-1)  24.5 us
    ppermute x8, starting transfers between devices, extended(): before = lax.ppermute(last, axis, up)  18.3 us
    concatenate x8, other arithmetic, extended(): value = jnp.concatenate([before, value, after], axis=dim)  16.8 us
    slice x8, local copies, waits for them, and re-layouts, body(): moved = [padded[1:-1, 2:], padded[1:-1, :-2]]  15.9 us
    concatenate x8, local copies, waits for them, and re-layouts, body(): moved.append(jnp.roll(center, -1, axis_number))  15 us
  transfers between devices with their start and end apart: 16, of which 10 were waited for; matrix products, arithmetic and copies ran while one was open for 40% of the time, Pallas kernels for 0%

commit v1 on v0

v1 whole, which is shorter than its diff:
```python
import functools

import jax
import jax.numpy as jnp
from jax import lax
from jax.experimental import pallas as pl
from jax.experimental.pallas import tpu as pltpu
from jax.sharding import PartitionSpec as P

MESH = pl.DeviceIdType.MESH
STEPS = 4
CHUNKS = 2
SITES = 16
PLANE = 8
BLOCKS = 8

SHIFT = 1.5
CENTER = 1.5
HALF_WIDTH = 1.0


def coefficients():
    ratio = HALF_WIDTH / CENTER
    pairs = [None]
    for _ in range(1, STEPS):
        following = 1.0 / (2.0 * CENTER / HALF_WIDTH - ratio)
        pairs.append((following * ratio, 2.0 * following / HALF_WIDTH))
        ratio = following
    return pairs


def kernel(
    r_hbm, self_hbm, hop_hbm, corr, res,
    raw_self, raw_hop, weights, v, ht, hx, direction,
    load_sem, v_sem, send_sem, recv_sem,
):
    groups, times = lax.axis_size("group"), lax.axis_size("site")
    g, t = lax.axis_index("group"), lax.axis_index("site")
    g_up, g_down = lax.rem(g + 1, groups), lax.rem(g + groups - 1, groups)
    t_up, t_down = lax.rem(t + 1, times), lax.rem(t + times - 1, times)
    rows = v.shape[3]
    coefs = coefficients()

    first = g * SITES
    load_self = pltpu.make_async_copy(
        self_hbm.at[0, pl.ds(first, SITES)], raw_self, load_sem.at[0]
    )
    load_hop = pltpu.make_async_copy(
        hop_hbm.at[0, pl.ds(first, SITES)], raw_hop, load_sem.at[1]
    )
    load_hop.start()
    load_self.start()

    def load_v(c):
        return pltpu.make_async_copy(
            r_hbm.at[0, :, pl.ds(c * rows, rows)], v.at[0, c], v_sem.at[c]
        )

    for c in range(CHUNKS):
        load_v(c).start()

    def sends(k, c):
        mine = v.at[k, c]
        targets = (
            (mine, ht.at[k, c, 0], (g, t_down)),
            (mine, ht.at[k, c, 1], (g, t_up)),
            (mine.at[pl.ds(0, PLANE)], hx.at[k, c, 0], (g_down, t)),
            (mine.at[pl.ds(PLANE, PLANE)], hx.at[k, c, 1], (g_up, t)),
        )
        return [
            pltpu.make_async_remote_copy(
                src_ref=src,
                dst_ref=dst,
                send_sem=send_sem.at[k, c, i],
                recv_sem=recv_sem.at[k, c, i],
                device_id=device,
                device_id_type=MESH,
            )
            for i, (src, dst, device) in enumerate(targets)
        ]

    barrier = pltpu.get_barrier_semaphore()
    for device in ((g, t_down), (g, t_up), (g_down, t), (g_up, t)):
        pl.semaphore_signal(barrier, inc=1, device_id=device, device_id_type=MESH)
    pl.semaphore_wait(barrier, 4)

    for c in range(CHUNKS):
        load_v(c).wait()
        for copy in sends(0, c):
            copy.start()

    load_self.wait()
    load_hop.wait()
    sign = jnp.where(
        lax.broadcasted_iota(jnp.int32, (64, 128), 1) < 64, 1.0, -1.0
    ).astype(jnp.float32)

    def build(s, carry):
        hop = [raw_hop[s, m].astype(jnp.float32) for m in range(8)]
        blocks = [raw_self[s].astype(jnp.float32), hop[4] + hop[5]]
        blocks += [hop[m] for m in (0, 1, 2, 3, 6, 7)]
        for m, block in enumerate(blocks):
            weights[s, 0:64, m * 128 : (m + 1) * 128] = (block * sign).astype(jnp.bfloat16)
            weights[s, 64:128, m * 128 : (m + 1) * 128] = pltpu.roll(
                block, 64, 1
            ).astype(jnp.bfloat16)
        return carry

    lax.fori_loop(0, SITES, build, 0)

    def compute(k, c):
        def position(p, carry):
            partner = p + 1 - 2 * lax.rem(p, 2)
            y_up, y_down = lax.rem(p + 2, PLANE), lax.rem(p + 6, PLANE)
            for x in range(2):
                base = x * PLANE
                s = base + p
                own = v[k, c, s]
                x_up = v[k, c, PLANE + p] if x == 0 else hx[k, c, 0, p]
                x_down = hx[k, c, 1, p] if x == 0 else v[k, c, p]
                lhs = jnp.concatenate(
                    [
                        own,
                        v[k, c, base + partner],
                        x_up,
                        x_down,
                        v[k, c, base + y_up],
                        v[k, c, base + y_down],
                        ht[k, c, 0, s],
                        ht[k, c, 1, s],
                    ],
                    axis=-1,
                )
                mixed = lax.dot_general(
                    lhs,
                    weights[s],
                    (((1,), (1,)), ((), ())),
                    preferred_element_type=jnp.float32,
                )
                here = pl.ds(c * rows, rows)
                wide = own.astype(jnp.float32)
                if k == 0:
                    residual = mixed * (-1.0 / CENTER)
                    before = wide * (1.0 / CENTER)
                    total = before
                else:
                    residual = res[0, s, here, :] - SHIFT * wide - mixed
                    if k < STEPS - 1:
                        before = direction[c, s]
                        total = corr[0, s, here, :]
                res[0, s, here, :] = residual
                if k < STEPS - 1:
                    scale, gain = coefs[k + 1]
                    now = scale * before + gain * residual
                    direction[c, s] = now
                    corr[0, s, here, :] = total + now
                    v[k + 1, c, s] = now.astype(jnp.bfloat16)
            return carry

        lax.fori_loop(0, PLANE, position, 0)

    for k in range(STEPS):
        for c in range(CHUNKS):
            for copy in sends(k, c):
                copy.wait_recv()
            compute(k, c)
            if k < STEPS - 1:
                for copy in sends(k + 1, c):
                    copy.start()
    for k in range(STEPS):
        for c in range(CHUNKS):
            for copy in sends(k, c):
                copy.wait_send()


def body(residual_in, self_block, hop_blocks):
    count = residual_in.shape[2]
    rows = count // CHUNKS
    out = jax.ShapeDtypeStruct(residual_in.shape, jnp.float32)
    any_space = pl.BlockSpec(memory_space=pl.ANY)
    vmem = pl.BlockSpec(memory_space=pltpu.VMEM)
    return pl.pallas_call(
        kernel,
        out_shape=(out, out),
        in_specs=[any_space] * 3,
        out_specs=(vmem, vmem),
        scratch_shapes=[
            pltpu.VMEM((SITES, 64, 128), jnp.bfloat16),
            pltpu.VMEM((SITES, 8, 64, 128), jnp.bfloat16),
            pltpu.VMEM((SITES, 128, BLOCKS * 128), jnp.bfloat16),
            pltpu.VMEM((STEPS, CHUNKS, SITES, rows, 128), jnp.bfloat16),
            pltpu.VMEM((STEPS, CHUNKS, 2, SITES, rows, 128), jnp.bfloat16),
            pltpu.VMEM((STEPS, CHUNKS, 2, PLANE, rows, 128), jnp.bfloat16),
            pltpu.VMEM((CHUNKS, SITES, rows, 128), jnp.float32),
            pltpu.SemaphoreType.DMA((2,)),
            pltpu.SemaphoreType.DMA((CHUNKS,)),
            pltpu.SemaphoreType.DMA((STEPS, CHUNKS, 4)),
            pltpu.SemaphoreType.DMA((STEPS, CHUNKS, 4)),
        ],
        compiler_params=pltpu.CompilerParams(
            collective_id=0,
            has_side_effects=True,
            vmem_limit_bytes=48 * 1024 * 1024,
        ),
        name="smoother",
    )(residual_in, self_block, hop_blocks)


def solution(mesh):
    return jax.shard_map(
        body,
        mesh=mesh,
        in_specs=(
            P("site", "group", None, None),
            P("site", None, None, None),
            P("site", None, None, None, None),
        ),
        out_specs=(P("site", "group", None, None), P("site", "group", None, None)),
        check_vma=False,
    )
```

time: 286 us -> 86.9 us (0.30); the launches traced: 281 us -> 86.7 us
  local copies, waits for them, and re-layouts: 127 us -> 4.2 us
  Pallas kernels: 0 us -> 81.9 us
  other arithmetic: 58.1 us -> 0 us
  waiting for transfers between devices: 35.1 us -> 0 us
  starting transfers between devices: 30.4 us -> 0 us
  matrix products: 29.2 us -> 0 us
    pallas_call x0 -> x1, Pallas kernels: none -> 81.9 us  [body(): pl.pallas_call(kernel, out_shape=(out, out), in_specs=[any_space] * 3, ou...]
    slice x44 -> x0, local copies, waits for them, and re-layouts: 47.3 us -> none  [the longest x8 15.9 us: body(): moved = [padded[1:-1, 2:], padded[1:-1, :-2]]]
    unnamed x71 -> x6, local copies, waits for them, and re-layouts: 51.1 us -> 4.2 us
    ppermute x16 -> x0, waiting for transfers between devices: 35.1 us -> none  [the longest x8 24.7 us: extended(): after = lax.ppermute(leading, axis, down)]
    ppermute x16 -> x0, starting transfers between devices: 30.4 us -> none  [the longest x8 18.3 us: extended(): before = lax.ppermute(last, axis, up)]
    dot_general x8 -> x0, matrix products: 29.2 us -> none  [the longest x4 28 us: apply_blocks(): jnp.einsum('tsmab,tsmkb->tska', own_hops, paired(around), preferred_eleme...]
    concatenate x19 -> x0, other arithmetic: 28.8 us -> none  [the longest x8 16.8 us: extended(): value = jnp.concatenate([before, value, after], axis=dim)]
    neg x8 -> x0, other arithmetic: 24.5 us -> none  [paired(): conjugate = jnp.concatenate([real_part, -imag_part], axis=-1)]
  transfers between devices with their start and end apart: 16 -> 0, of which waited for: 10 -> 0; matrix products, arithmetic and copies ran while one was open for 40% -> 0% of each run, Pallas kernels for 0% -> 0%
where the time goes in v1:
time: 86.9 us; the launch traced here: 86.7 us
  Pallas kernels  81.9 us (94%)
  local copies, waits for them, and re-layouts  4.2 us (5%)
    pallas_call x1, Pallas kernels, body(): pl.pallas_call(kernel, out_shape=(out, out), in_specs=[any_space] * 3, ou...  81.9 us
    unnamed x6, local copies, waits for them, and re-layouts  4.2 us

profile of v1, /device:TPU:1, one launch (start us, length us, event | category | flops | bytes accessed | tf_op | source)
XLA Modules:
  0.0 86.7 jit_solution(628682248326470438)
XLA Ops:
  0.6 0.0 copy-start
  0.6 1.2 %copy-done = bf16[1,64,64,128]{3,2,1,0:T(8,128)(2,1)S(1)} copy-done((bf16[1,64,64,128]{3,2,1,0:T(8,128)(2,1)S(1)}, bf16[1,64,64,128]{3,2,1,0:T(8,128)(2,1)}, u32[]{:S(2)}) %copy-start) | copy-done | bytes 1048600
  1.9 0.0 copy-start.1
  1.9 1.0 %copy-done.1 = bf16[1,16,128,128]{3,2,1,0:T(8,128)(2,1)S(1)} copy-done((bf16[1,16,128,128]{3,2,1,0:T(8,128)(2,1)S(1)}, bf16[1,16,128,128]{3,2,1,0:T(8,128)(2,1)}, u32[]{:S(2)}) %copy-start.1) | copy-done | bytes 524312
  2.9 81.9 %smoother.1 = (f32[1,16,128,128]{3,2,1,0:T(8,128)S(1)}, f32[1,16,128,128]{3,2,1,0:T(8,128)S(1)}) custom-call(bf16[1,16,128,128]{3,2,1,0:T(8,128)(2,1)S(1)} %copy-done.1, bf16[1,64,64,128]{3,2,1,0:T(8,128)(2,1)S(1)} %copy-done, bf16[1,64,8,64,128]{4,3,2,1,0:T(8,128)(2,1)} %hop_hbm.1), custom_call_target="tpu_custom_call" | custom-call | tf_op jit(solution)/shard_map/smoother/pallas_call | solution.py:182
  84.8 1.0 %copy.7 = f32[1,16,128,128]{3,2,1,0:T(8,128)} copy(f32[1,16,128,128]{3,2,1,0:T(8,128)S(1)} %get-tuple-element.4) | data formatting | bytes 2097152
  85.8 1.0 %copy.8 = f32[1,16,128,128]{3,2,1,0:T(8,128)} copy(f32[1,16,128,128]{3,2,1,0:T(8,128)S(1)} %get-tuple-element.5) | data formatting | bytes 2097152
Async XLA Ops:
  0.6 1.2 %copy-start = (bf16[1,64,64,128]{3,2,1,0:T(8,128)(2,1)S(1)}, bf16[1,64,64,128]{3,2,1,0:T(8,128)(2,1)}, u32[]{:S(2)}) copy-start(bf16[1,64,64,128]{3,2,1,0:T(8,128)(2,1)} %self_hbm.1) | copy-start | bytes 3145732
  1.9 1.0 %copy-start.1 = (bf16[1,16,128,128]{3,2,1,0:T(8,128)(2,1)S(1)}, bf16[1,16,128,128]{3,2,1,0:T(8,128)(2,1)}, u32[]{:S(2)}) copy-start(bf16[1,16,128,128]{3,2,1,0:T(8,128)(2,1)} %r_hbm.1) | copy-start | bytes 1572868

commit v2 on v0

v2 whole, which is shorter than its diff:
```python
import functools

import jax
import jax.numpy as jnp
from jax import lax
from jax.experimental import pallas as pl
from jax.experimental.pallas import tpu as pltpu
from jax.sharding import PartitionSpec as P

MESH = pl.DeviceIdType.MESH
STEPS = 4
SITES = 16
PLANE = 8
BLOCKS = 8
SIZE = 2
GROUPS = SITES // SIZE
WRAP = 16
RELAY = True

SHIFT = 1.5
CENTER = 1.5
HALF_WIDTH = 1.0


def coefficients():
    ratio = HALF_WIDTH / CENTER
    pairs = [None]
    for _ in range(1, STEPS):
        following = 1.0 / (2.0 * CENTER / HALF_WIDTH - ratio)
        pairs.append((following * ratio, 2.0 * following / HALF_WIDTH))
        ratio = following
    return pairs


def relayed(j):
    return RELAY and j % 2 == 1


def kernel(
    r_hbm, self_hbm, hop_hbm, corr, res,
    raw_self, raw_hop, weights, v, ht, hx, passing, direction,
    load_sem, send_sem, recv_sem, pass_sem, forward_sem,
):
    groups, times = lax.axis_size("group"), lax.axis_size("site")
    g, t = lax.axis_index("group"), lax.axis_index("site")
    odd = lax.rem(g, 2)
    other_chip = lax.rem(g + groups - 1 + 2 * odd, groups)
    other_core = g + 1 - 2 * odd
    t_up, t_down = lax.rem(t + 1, times), lax.rem(t + times - 1, times)
    place = lax.rem(t, WRAP)
    coefs = coefficients()
    base = (odd * PLANE, PLANE - odd * PLANE)

    def loads():
        copies = []
        for role in range(2):
            here, there = pl.ds(role * PLANE, PLANE), pl.ds(base[role], PLANE)
            far = pl.ds(g * SITES + base[role], PLANE)
            copies += [
                (hop_hbm.at[0, far], raw_hop.at[here]),
                (self_hbm.at[0, far], raw_self.at[here]),
                (r_hbm.at[0, there], v.at[0, here]),
            ]
        return [
            pltpu.make_async_copy(src, dst, load_sem.at[i])
            for i, (src, dst) in enumerate(copies)
        ]

    for copy in loads():
        copy.start()

    def remote(src, dst, send, recv, device):
        return pltpu.make_async_remote_copy(
            src_ref=src,
            dst_ref=dst,
            send_sem=send,
            recv_sem=recv,
            device_id=device,
            device_id_type=MESH,
        )

    def faces(k, j):
        role, inside = divmod(j, GROUPS // 2)
        here = pl.ds(j * SIZE, SIZE)
        if k == 0:
            mine = r_hbm.at[0, pl.ds(base[role] + inside * SIZE, SIZE)]
        else:
            mine = v.at[k, here]
        partner = other_core if role else other_chip
        landing = hx.at[k, role, pl.ds(inside * SIZE, SIZE)]
        targets = (
            (ht.at[k, 0, here], (g, t_down)),
            (ht.at[k, 1, here], (g, t_up)),
            (landing, (partner, t)),
        )
        return [
            remote(mine, dst, send_sem.at[k, j, i], recv_sem.at[k, j, i], device)
            for i, (dst, device) in enumerate(targets)
        ], mine

    def send(k, j):
        copies, mine = faces(k, j)
        if relayed(j):
            for i, edge, step in ((0, 0, 3), (1, WRAP - 1, -3)):
                detour = remote(
                    mine,
                    passing.at[k, j // 2],
                    send_sem.at[k, j, i],
                    pass_sem.at[k, j // 2],
                    (g, t + step),
                )

                @pl.when(place == edge)
                def _(detour=detour):
                    detour.start()

                @pl.when(place != edge)
                def _(direct=copies[i]):
                    direct.start()

        else:
            copies[0].start()
            copies[1].start()
        copies[2].start()

    def forwards(k, j):
        here = pl.ds(j * SIZE, SIZE)
        out = []
        for i, spot, step in ((0, 3, times - 4), (1, WRAP - 4, 4)):
            out.append((
                spot,
                remote(
                    passing.at[k, j // 2],
                    ht.at[k, i, here],
                    forward_sem.at[k, j // 2],
                    recv_sem.at[k, j, i],
                    (g, lax.rem(t + step, times)),
                ),
                remote(
                    passing.at[k, j // 2],
                    passing.at[k, j // 2],
                    forward_sem.at[k, j // 2],
                    pass_sem.at[k, j // 2],
                    (g, t_up),
                ),
            ))
        return out

    def forward(k, j):
        if relayed(j):
            for spot, onward, arrival in forwards(k, j):

                @pl.when(place == spot)
                def _(onward=onward, arrival=arrival):
                    arrival.wait_recv()
                    onward.start()

    barrier = pltpu.get_barrier_semaphore()

    def greet(device):
        pl.semaphore_signal(barrier, inc=1, device_id=device, device_id_type=MESH)

    for device in ((g, t_down), (g, t_up), (other_chip, t), (other_core, t)):
        greet(device)
    guests = 4
    if RELAY:
        greetings = (
            (0, lax.rem(t + times - 4, times)),
            (WRAP - 1, lax.rem(t + 4, times)),
            (3, t - 3),
            (WRAP - 4, t + 3),
        )
        for spot, device in greetings:
            guests += jnp.where(place == spot, 1, 0)

            @pl.when(place == spot)
            def _(device=device):
                greet((g, device))

    pl.semaphore_wait(barrier, guests)

    for j in range(GROUPS):
        send(0, j)
    for copy in loads():
        copy.wait()

    sign = jnp.where(
        lax.broadcasted_iota(jnp.int32, (64, 128), 1) < 64, 1.0, -1.0
    ).astype(jnp.float32)

    def build(role):
        plane = odd if role == 0 else 1 - odd

        def one(p, carry):
            s = role * PLANE + p

            def hop(m):
                return raw_hop[s, m].astype(jnp.float32)

            blocks = [
                raw_self[s].astype(jnp.float32),
                hop(4) + hop(5),
                hop(plane),
                hop(1 - plane),
                hop(2),
                hop(3),
                hop(6),
                hop(7),
            ]
            for m, block in enumerate(blocks):
                full = jnp.concatenate([block * sign, pltpu.roll(block, 64, 1)], axis=0)
                weights[s, m * 128 : (m + 1) * 128, :] = full.T.astype(jnp.bfloat16)
            return carry

        lax.fori_loop(0, PLANE, one, 0)

    build(0)
    build(1)

    def compute(k, j):
        role, inside = divmod(j, GROUPS // 2)

        def one(p):
            s = role * PLANE + p
            partner = p + 1 if p % 2 == 0 else p - 1
            own = v[k, s]
            lhs = jnp.concatenate(
                [
                    own,
                    v[k, role * PLANE + partner],
                    v[k, (1 - role) * PLANE + p],
                    hx[k, role, p],
                    v[k, role * PLANE + (p + 2) % PLANE],
                    v[k, role * PLANE + (p + 6) % PLANE],
                    ht[k, 0, s],
                    ht[k, 1, s],
                ],
                axis=-1,
            )
            mixed = jnp.dot(lhs, weights[s], preferred_element_type=jnp.float32)
            out = base[role] + p
            wide = own.astype(jnp.float32)
            if k == 0:
                residual = mixed * (-1.0 / CENTER)
                before = wide * (1.0 / CENTER)
                total = before
            else:
                residual = res[0, out] - SHIFT * wide - mixed
                if k < STEPS - 1:
                    before = direction[s]
                    total = corr[0, out]
            res[0, out] = residual
            if k < STEPS - 1:
                scale, gain = coefs[k + 1]
                now = scale * before + gain * residual
                direction[s] = now
                corr[0, out] = total + now
                v[k + 1, s] = now.astype(jnp.bfloat16)

        for p in range(inside * SIZE, (inside + 1) * SIZE):
            one(p)

    for k in range(STEPS):
        for j in range(GROUPS):
            for copy in faces(k, j)[0]:
                copy.wait_recv()
            forward(k, j)
            compute(k, j)
            if k < STEPS - 1:
                send(k + 1, j)
    for k in range(STEPS):
        for j in range(GROUPS):
            for copy in faces(k, j)[0]:
                copy.wait_send()
            if relayed(j):
                for spot, onward, _ in forwards(k, j):

                    @pl.when(place == spot)
                    def _(onward=onward):
                        onward.wait_send()


def store(corr_in, res_in, corr_out, res_out, sems):
    parts = 4
    size = SITES // parts
    copies = []
    for a, (src, dst) in enumerate(((corr_in, corr_out), (res_in, res_out))):
        for i in range(parts):
            here = pl.ds(i * size, size)
            copies.append(
                pltpu.make_async_copy(src.at[0, here], dst.at[0, here], sems.at[a, i])
            )
    for copy in copies:
        copy.start()
    for copy in copies:
        copy.wait()


def body(residual_in, self_block, hop_blocks):
    out = jax.ShapeDtypeStruct(residual_in.shape, jnp.float32)
    hbm = pl.BlockSpec(memory_space=pltpu.HBM)
    vmem = pl.BlockSpec(memory_space=pltpu.VMEM)
    tile = (128, 128)
    results = pl.pallas_call(
        kernel,
        out_shape=(out, out),
        in_specs=[hbm] * 3,
        out_specs=(vmem, vmem),
        scratch_shapes=[
            pltpu.VMEM((SITES, 64, 128), jnp.bfloat16),
            pltpu.VMEM((SITES, 8, 64, 128), jnp.bfloat16),
            pltpu.VMEM((SITES, BLOCKS * 128, 128), jnp.bfloat16),
            pltpu.VMEM((STEPS, SITES) + tile, jnp.bfloat16),
            pltpu.VMEM((STEPS, 2, SITES) + tile, jnp.bfloat16),
            pltpu.VMEM((STEPS, 2, PLANE) + tile, jnp.bfloat16),
            pltpu.VMEM((STEPS, GROUPS // 2, SIZE) + tile, jnp.bfloat16),
            pltpu.VMEM((SITES,) + tile, jnp.float32),
            pltpu.SemaphoreType.DMA((6,)),
            pltpu.SemaphoreType.DMA((STEPS, GROUPS, 3)),
            pltpu.SemaphoreType.DMA((STEPS, GROUPS, 3)),
            pltpu.SemaphoreType.DMA((STEPS, GROUPS // 2)),
            pltpu.SemaphoreType.DMA((STEPS, GROUPS // 2)),
        ],
        compiler_params=pltpu.CompilerParams(
            collective_id=0,
            has_side_effects=True,
            vmem_limit_bytes=48 * 1024 * 1024,
        ),
        name="smoother",
    )(*(pltpu.with_memory_space_constraint(x, pltpu.HBM) for x in (residual_in, self_block, hop_blocks)))
    return pl.pallas_call(
        store,
        out_shape=(out, out),
        in_specs=[pl.BlockSpec(memory_space=pl.ANY)] * 2,
        out_specs=(hbm, hbm),
        scratch_shapes=[pltpu.SemaphoreType.DMA((2, 4))],
        name="store",
    )(*(pltpu.with_memory_space_constraint(x, pltpu.VMEM) for x in results))


def solution(mesh):
    return jax.shard_map(
        body,
        mesh=mesh,
        in_specs=(
            P("site", "group", None, None),
            P("site", None, None, None),
            P("site", None, None, None, None),
        ),
        out_specs=(P("site", "group", None, None), P("site", "group", None, None)),
        check_vma=False,
    )
```

time: 286 us -> 68.6 us (0.24)
  the two profiles are of different devices: /device:TPU:1 before, /device:TPU:4 now
where the time goes in v2:
time: 68.6 us; the launch traced here: 68.5 us
  Pallas kernels  67.9 us (99%)
    pallas_call x1, Pallas kernels, body(): pl.pallas_call(kernel, out_shape=(out, out), in_specs=[hbm] * 3, out_spec...  66.5 us
    pallas_call x1, Pallas kernels, body(): pl.pallas_call(store, out_shape=(out, out), in_specs=[pl.BlockSpec(memory...  1.38 us

profile of v2, /device:TPU:4, one launch (start us, length us, event | category | flops | bytes accessed | tf_op | source)
XLA Modules:
  0.0 68.5 jit_solution(14110542278204866913)
XLA Ops:
  0.6 66.5 %smoother.1 = (f32[1,16,128,128]{3,2,1,0:T(8,128)S(1)}, f32[1,16,128,128]{3,2,1,0:T(8,128)S(1)}) custom-call(bf16[1,16,128,128]{3,2,1,0:T(8,128)(2,1)} %r_hbm.1, bf16[1,64,64,128]{3,2,1,0:T(8,128)(2,1)} %self_hbm.1, bf16[1,64,8,64,128]{4,3,2,1,0:T(8,128)(2,1)} %hop_hbm.1), custom_call_target="tpu_custom_call" | custom-call | tf_op jit(solution)/shard_map/smoother/pallas_call | solution.py:304
  67.2 1.4 %store.1 = (f32[1,16,128,128]{3,2,1,0:T(8,128)}, f32[1,16,128,128]{3,2,1,0:T(8,128)}) custom-call(f32[1,16,128,128]{3,2,1,0:T(8,128)S(1)} %get-tuple-element.4.corr_in, f32[1,16,128,128]{3,2,1,0:T(8,128)S(1)} %get-tuple-element.5.res_in), custom_call_target="tpu_custom_call" | custom-call | tf_op jit(solution)/shard_map/store/pallas_call | solution.py:331

commit v3 on v2

--- a/solution.py
+++ b/solution.py
@@ -32,8 +32,11 @@
     return pairs
 
 
-def relayed(j):
-    return RELAY and j % 2 == 1
+ORDERS = ((0, 2, 1, 4, 3, 6, 5, 7), (1, 0, 3, 2, 5, 4, 7, 6))
+
+
+def relayed(k, j):
+    return RELAY and (j + k) % 2 == 1
 
 
 def kernel(
@@ -62,7 +65,7 @@
                 (r_hbm.at[0, there], v.at[0, here]),
             ]
         return [
-            pltpu.make_async_copy(src, dst, load_sem.at[i])
+            pltpu.make_async_copy(src, dst, load_sem.at[i % 3])
             for i, (src, dst) in enumerate(copies)
         ]
 
@@ -94,18 +97,18 @@
             (landing, (partner, t)),
         )
         return [
-            remote(mine, dst, send_sem.at[k, j, i], recv_sem.at[k, j, i], device)
+            remote(mine, dst, send_sem.at[k, i // 2], recv_sem.at[k, j], device)
             for i, (dst, device) in enumerate(targets)
         ], mine
 
     def send(k, j):
         copies, mine = faces(k, j)
-        if relayed(j):
+        if relayed(k, j):
             for i, edge, step in ((0, 0, 3), (1, WRAP - 1, -3)):
                 detour = remote(
                     mine,
                     passing.at[k, j // 2],
-                    send_sem.at[k, j, i],
+                    send_sem.at[k, 0],
                     pass_sem.at[k, j // 2],
                     (g, t + step),
                 )
@@ -132,14 +135,14 @@
                 remote(
                     passing.at[k, j // 2],
                     ht.at[k, i, here],
-                    forward_sem.at[k, j // 2],
-                    recv_sem.at[k, j, i],
+                    forward_sem.at[k],
+                    recv_sem.at[k, j],
                     (g, lax.rem(t + step, times)),
                 ),
                 remote(
                     passing.at[k, j // 2],
                     passing.at[k, j // 2],
-                    forward_sem.at[k, j // 2],
+                    forward_sem.at[k],
                     pass_sem.at[k, j // 2],
                     (g, t_up),
                 ),
@@ -147,7 +150,7 @@
         return out
 
     def forward(k, j):
-        if relayed(j):
+        if relayed(k, j):
             for spot, onward, arrival in forwards(k, j):
 
                 @pl.when(place == spot)
@@ -179,10 +182,15 @@
 
     pl.semaphore_wait(barrier, guests)
 
-    for j in range(GROUPS):
+    for j in ORDERS[1]:
         send(0, j)
-    for copy in loads():
-        copy.wait()
+    whole = (
+        (hop_hbm.at[0, pl.ds(0, SITES)], raw_hop),
+        (self_hbm.at[0, pl.ds(0, SITES)], raw_self),
+        (r_hbm.at[0], v.at[0]),
+    )
+    for i, (src, dst) in enumerate(whole):
+        pltpu.make_async_copy(src, dst, load_sem.at[i]).wait()
 
     sign = jnp.where(
         lax.broadcasted_iota(jnp.int32, (64, 128), 1) < 64, 1.0, -1.0
@@ -260,24 +268,29 @@
         for p in range(inside * SIZE, (inside + 1) * SIZE):
             one(p)
 
+    def all_bytes(ref, send, recv):
+        return remote(ref, ref, send, recv, (g, t_up))
+
     for k in range(STEPS):
-        for j in range(GROUPS):
-            for copy in faces(k, j)[0]:
-                copy.wait_recv()
-            forward(k, j)
+        waiting = [j for j in range(GROUPS) if relayed(k, j)]
+        for place_in_step, j in enumerate(ORDERS[k % 2]):
+            if place_in_step % 2 == 0 and waiting:
+                forward(k, waiting.pop(0))
+            three = v.at[k, pl.ds(0, 3 * SIZE)]
+            all_bytes(three, send_sem.at[k, 0], recv_sem.at[k, j]).wait_recv()
             compute(k, j)
             if k < STEPS - 1:
                 send(k + 1, j)
     for k in range(STEPS):
-        for j in range(GROUPS):
-            for copy in faces(k, j)[0]:
-                copy.wait_send()
-            if relayed(j):
-                for spot, onward, _ in forwards(k, j):
-
-                    @pl.when(place == spot)
-                    def _(onward=onward):
-                        onward.wait_send()
+        all_bytes(ht.at[k], send_sem.at[k, 0], recv_sem.at[k, 0]).wait_send()
+        all_bytes(v.at[k], send_sem.at[k, 1], recv_sem.at[k, 0]).wait_send()
+    if RELAY:
+
+        @pl.when((place == 3) | (place == WRAP - 4))
+        def _():
+            for k in range(STEPS):
+                half = v.at[k, pl.ds(0, SITES // 2)]
+                all_bytes(half, forward_sem.at[k], recv_sem.at[k, 0]).wait_send()
 
 
 def store(corr_in, res_in, corr_out, res_out, sems):
@@ -315,11 +328,11 @@
             pltpu.VMEM((STEPS, 2, PLANE) + tile, jnp.bfloat16),
             pltpu.VMEM((STEPS, GROUPS // 2, SIZE) + tile, jnp.bfloat16),
             pltpu.VMEM((SITES,) + tile, jnp.float32),
-            pltpu.SemaphoreType.DMA((6,)),
-            pltpu.SemaphoreType.DMA((STEPS, GROUPS, 3)),
-            pltpu.SemaphoreType.DMA((STEPS, GROUPS, 3)),
+            pltpu.SemaphoreType.DMA((3,)),
+            pltpu.SemaphoreType.DMA((STEPS, 2)),
+            pltpu.SemaphoreType.DMA((STEPS, GROUPS)),
             pltpu.SemaphoreType.DMA((STEPS, GROUPS // 2)),
-            pltpu.SemaphoreType.DMA((STEPS, GROUPS // 2)),
+            pltpu.SemaphoreType.DMA((STEPS,)),
         ],
         compiler_params=pltpu.CompilerParams(
             collective_id=0,

time: 68.6 us -> 64.6 us (0.942)
  the two profiles are of different devices: /device:TPU:4 before, /device:TPU:1 now
where the time goes in v3:
time: 64.6 us; the launch traced here: 64.5 us
  Pallas kernels  63.9 us (99%)
    pallas_call x1, Pallas kernels, body(): pl.pallas_call(kernel, out_shape=(out, out), in_specs=[hbm] * 3, out_spec...  62.5 us
    pallas_call x1, Pallas kernels, body(): pl.pallas_call(store, out_shape=(out, out), in_specs=[pl.BlockSpec(memory...  1.38 us

profile of v3, /device:TPU:1, one launch (start us, length us, event | category | flops | bytes accessed | tf_op | source)
XLA Modules:
  0.0 64.5 jit_solution(9533373238280815454)
XLA Ops:
  0.6 62.5 %smoother.1 = (f32[1,16,128,128]{3,2,1,0:T(8,128)S(1)}, f32[1,16,128,128]{3,2,1,0:T(8,128)S(1)}) custom-call(bf16[1,16,128,128]{3,2,1,0:T(8,128)(2,1)} %r_hbm.1, bf16[1,64,64,128]{3,2,1,0:T(8,128)(2,1)} %self_hbm.1, bf16[1,64,8,64,128]{4,3,2,1,0:T(8,128)(2,1)} %hop_hbm.1), custom_call_target="tpu_custom_call" | custom-call | tf_op jit(solution)/shard_map/smoother/pallas_call | solution.py:317
  63.1 1.4 %store.1 = (f32[1,16,128,128]{3,2,1,0:T(8,128)}, f32[1,16,128,128]{3,2,1,0:T(8,128)}) custom-call(f32[1,16,128,128]{3,2,1,0:T(8,128)S(1)} %get-tuple-element.4.corr_in, f32[1,16,128,128]{3,2,1,0:T(8,128)S(1)} %get-tuple-element.5.res_in), custom_call_target="tpu_custom_call" | custom-call | tf_op jit(solution)/shard_map/store/pallas_call | solution.py:344

commit v4 on v3

--- a/solution.py
+++ b/solution.py
@@ -274,7 +274,7 @@
     for k in range(STEPS):
         waiting = [j for j in range(GROUPS) if relayed(k, j)]
         for place_in_step, j in enumerate(ORDERS[k % 2]):
-            if place_in_step % 2 == 0 and waiting:
+            if waiting:
                 forward(k, waiting.pop(0))
             three = v.at[k, pl.ds(0, 3 * SIZE)]
             all_bytes(three, send_sem.at[k, 0], recv_sem.at[k, j]).wait_recv()

time: 64.6 us -> 64.2 us (level)
  no operation moved by 1% of the time
where the time goes in v4:
time: 64.2 us; the launch traced here: 64 us
  Pallas kernels  63.4 us (99%)
    pallas_call x1, Pallas kernels, body(): pl.pallas_call(kernel, out_shape=(out, out), in_specs=[hbm] * 3, out_spec...  62 us
    pallas_call x1, Pallas kernels, body(): pl.pallas_call(store, out_shape=(out, out), in_specs=[pl.BlockSpec(memory...  1.38 us

profile of v4, /device:TPU:1, one launch (start us, length us, event | category | flops | bytes accessed | tf_op | source)
XLA Modules:
  0.0 64.0 jit_solution(233373192197666452)
XLA Ops:
  0.6 62.0 %smoother.1 = (f32[1,16,128,128]{3,2,1,0:T(8,128)S(1)}, f32[1,16,128,128]{3,2,1,0:T(8,128)S(1)}) custom-call(bf16[1,16,128,128]{3,2,1,0:T(8,128)(2,1)} %r_hbm.1, bf16[1,64,64,128]{3,2,1,0:T(8,128)(2,1)} %self_hbm.1, bf16[1,64,8,64,128]{4,3,2,1,0:T(8,128)(2,1)} %hop_hbm.1), custom_call_target="tpu_custom_call" | custom-call | tf_op jit(solution)/shard_map/smoother/pallas_call | solution.py:317
  62.7 1.4 %store.1 = (f32[1,16,128,128]{3,2,1,0:T(8,128)}, f32[1,16,128,128]{3,2,1,0:T(8,128)}) custom-call(f32[1,16,128,128]{3,2,1,0:T(8,128)S(1)} %get-tuple-element.4.corr_in, f32[1,16,128,128]{3,2,1,0:T(8,128)S(1)} %get-tuple-element.5.res_in), custom_call_target="tpu_custom_call" | custom-call | tf_op jit(solution)/shard_map/store/pallas_call | solution.py:344

commit v5 on v4

--- a/solution.py
+++ b/solution.py
@@ -274,7 +274,7 @@
     for k in range(STEPS):
         waiting = [j for j in range(GROUPS) if relayed(k, j)]
         for place_in_step, j in enumerate(ORDERS[k % 2]):
-            if waiting:
+            for _ in waiting[:2]:
                 forward(k, waiting.pop(0))
             three = v.at[k, pl.ds(0, 3 * SIZE)]
             all_bytes(three, send_sem.at[k, 0], recv_sem.at[k, j]).wait_recv()

time: 64.2 us -> 65.7 us (1.023)
  Pallas kernels: 63.4 us -> 64.5 us
    pallas_call x1, Pallas kernels: 62 us -> 63.1 us  [body(): pl.pallas_call(kernel, out_shape=(out, out), in_specs=[hbm] * 3, out_spec...]
where the time goes in v5:
time: 65.7 us; the launch traced here: 65.1 us
  Pallas kernels  64.5 us (98%)
    pallas_call x1, Pallas kernels, body(): pl.pallas_call(kernel, out_shape=(out, out), in_specs=[hbm] * 3, out_spec...  63.1 us
    pallas_call x1, Pallas kernels, body(): pl.pallas_call(store, out_shape=(out, out), in_specs=[pl.BlockSpec(memory...  1.38 us

profile of v5, /device:TPU:1, one launch (start us, length us, event | category | flops | bytes accessed | tf_op | source)
XLA Modules:
  0.0 65.1 jit_solution(9751629734081614315)
XLA Ops:
  0.6 63.1 %smoother.1 = (f32[1,16,128,128]{3,2,1,0:T(8,128)S(1)}, f32[1,16,128,128]{3,2,1,0:T(8,128)S(1)}) custom-call(bf16[1,16,128,128]{3,2,1,0:T(8,128)(2,1)} %r_hbm.1, bf16[1,64,64,128]{3,2,1,0:T(8,128)(2,1)} %self_hbm.1, bf16[1,64,8,64,128]{4,3,2,1,0:T(8,128)(2,1)} %hop_hbm.1), custom_call_target="tpu_custom_call" | custom-call | tf_op jit(solution)/shard_map/smoother/pallas_call | solution.py:317
  63.8 1.4 %store.1 = (f32[1,16,128,128]{3,2,1,0:T(8,128)}, f32[1,16,128,128]{3,2,1,0:T(8,128)}) custom-call(f32[1,16,128,128]{3,2,1,0:T(8,128)S(1)} %get-tuple-element.4.corr_in, f32[1,16,128,128]{3,2,1,0:T(8,128)S(1)} %get-tuple-element.5.res_in), custom_call_target="tpu_custom_call" | custom-call | tf_op jit(solution)/shard_map/store/pallas_call | solution.py:344
